TPU v7x, 128 devices: a whole 4x4x4 slice. The times are simulated.
128 devices in a mesh: group: 32 (over z, y, x_hi), head: 4 (over x_lo, core).
Axes of the slice: x: 4 (x_hi: 2, x_lo: 2; x = x_hi * 2 + x_lo), y: 4, z: 4, core: 2. Of those that a mesh axis runs over, the one named last changes fastest.
Arguments:
- tokens: bfloat16 [4, 4096, 1536], P(None, 'group'), may hold values from -6 to 6
- parents: int32 [3, 4096], P(None, 'group'), may hold values from 0 to 7
- page_request: int32 [1536], P('group'), may hold values from 0 to 511, as said below
- page_fill: int32 [1536], P('group'), may hold values from 1 to 128, as said below
- keys_pool: bfloat16 [1536, 1536, 128], P('group', 'head'), may hold values from -600 to 600
- values_pool: bfloat16 [1536, 1536, 128], P('group', 'head'), may hold values from -6 to 6
- decay_pool: bfloat16 [1536, 24, 128], P('group', 'head'), may hold values from -494.52 to 0
- gain_attn: float32 [1536], replicated, may hold values from 0.1 to 1.9
- w_query: bfloat16 [1536, 1536], P('head'), may hold values from -0.15625 to 0.15625
- w_key: bfloat16 [1536, 1536], P('head'), may hold values from -0.15625 to 0.15625
- w_value: bfloat16 [1536, 1536], P('head'), may hold values from -0.15625 to 0.15625
- w_forget: bfloat16 [1536, 24], P(None, 'head'), may hold values from -0.15625 to 0.15625
- forget_bias: float32 [24], P('head'), may hold values from -2 to 6
- w_out: bfloat16 [1536, 1536], P('head'), may hold values from -0.15625 to 0.15625
- gain_ffn: float32 [1536], replicated, may hold values from 0.1 to 1.9
- w_gate: bfloat16 [1536, 4096], P(None, 'head'), may hold values from -0.15625 to 0.15625
- w_up: bfloat16 [1536, 4096], P(None, 'head'), may hold values from -0.15625 to 0.15625
- w_down: bfloat16 [4096, 1536], P('head'), may hold values from -0.09375 to 0.09375
Outputs:
- outputs: bfloat16 [4, 4096, 1536], P(None, 'group')
Inputs may be any that keep to these rules, and one draw needn't show every extreme that they name: `page_request`: request ids g * 16 to g * 16 + 15 are the requests owned by group g, and pages g * 48 to g * 48 + 47 are the page slots of group g. The first 32 slots of a group hold pages of its own requests; its other 16 slots hold pages of other groups' requests, at most 1 from the requests of one group. Every request has at least one page. `page_fill`: the valid positions of a page are its first ones.
All inputs are finite; a program needn't handle non-finite values.
Results may differ from a plain program's by a relative error of at most 0.0095.
Values may be sent and summed in bfloat16 or wider, within the bound.
A program may use at most 192 MiB of HBM per device.

v0:
```python
import jax
import jax.numpy as jnp
from jax import lax
from jax.sharding import PartitionSpec as P

BEAMS = 8
OWNED_SLOTS = 32
SPILL = 16
epsilon = 1e-05
masked_score = -1e30


def rms_scale(values, gain_vector):
    widened = values.astype(jnp.float32)
    return (
        widened
        * lax.rsqrt(jnp.mean(widened * widened, axis=-1, keepdims=True) + epsilon)
        * gain_vector
    )


def page_partials(page_keys, page_values, page_decay, fill_count, asked_rows, head_count):
    page_count, inner_width, length = page_keys.shape
    head_size = inner_width // head_count
    keys_split = page_keys.reshape(page_count, head_count, head_size, length)
    values_split = page_values.reshape(page_count, head_count, head_size, length)
    asked_split = asked_rows.reshape(asked_rows.shape[:3] + (head_count, head_size))
    scores = jnp.einsum(
        "pbshd,phdt->pbsht", asked_split, keys_split, preferred_element_type=jnp.float32
    ) * head_size ** (-0.5)
    scores = scores + page_decay.astype(jnp.float32)[:, None, None, :, :]
    valid_mask = jnp.arange(length)[None, :] < fill_count[:, None]
    scores = jnp.where(valid_mask[:, None, None, None, :], scores, masked_score)
    page_top = jnp.max(scores, axis=-1)
    weights = jnp.exp(scores - page_top[..., None])
    page_total = jnp.sum(weights, axis=-1)
    numerator = jnp.einsum(
        "pbsht,phdt->pbshd",
        weights.astype(jnp.bfloat16),
        values_split,
        preferred_element_type=jnp.float32,
    )
    return (page_top, page_total, numerator.reshape(numerator.shape[:3] + (inner_width,)))


def by_request(current_request, page_top, page_total, numerator, request_count, head_count):
    matches = current_request[None, :] == jnp.arange(request_count)[:, None]
    wide_match = matches[:, :, None, None, None]
    best_top = jnp.max(jnp.where(wide_match, page_top[None], masked_score), axis=1)
    factor = jnp.where(wide_match, jnp.exp(page_top[None] - best_top[:, None]), 0.0)
    summed = jnp.sum(factor * page_total[None], axis=1)
    numer_split = numerator.reshape(numerator.shape[:3] + (head_count, -1))
    combined = jnp.sum(factor[..., None] * numer_split[None], axis=1)
    return (best_top, summed, combined.reshape(combined.shape[:3] + (-1,)))


def shards(
    tokens,
    parents,
    page_request,
    page_fill,
    keys_pool,
    values_pool,
    decay_pool,
    gain_attn,
    w_query,
    w_key,
    w_value,
    w_forget,
    forget_bias,
    w_out,
    gain_ffn,
    w_gate,
    w_up,
    w_down,
):
    step_count, row_count, model_width = tokens.shape
    head_count = w_forget.shape[1]
    inner_width = w_query.shape[0]
    head_size = inner_width // head_count
    local_count = row_count // BEAMS
    groups = lax.axis_size("group")
    own_group = lax.axis_index("group")
    capacity = (SPILL + groups - 2) // (groups - 1)
    flat_tokens = tokens.reshape(step_count * row_count, model_width)
    normed = rms_scale(flat_tokens, gain_attn).astype(jnp.bfloat16)

    def project(weight):
        product = lax.dot_general(
            normed, weight, (((1,), (1,)), ((), ())), preferred_element_type=jnp.float32
        )
        return product.astype(jnp.bfloat16).reshape(step_count, row_count, -1)

    queries = project(w_query)
    key_new = project(w_key)
    value_new = project(w_value)
    forget = jax.nn.log_sigmoid(
        jnp.dot(normed, w_forget, preferred_element_type=jnp.float32) + forget_bias
    ).reshape(step_count, row_count, head_count)
    by_row = queries.transpose(1, 0, 2)
    by_request_rows = by_row.reshape(local_count, BEAMS, step_count, inner_width)
    own_request = page_request[:OWNED_SLOTS] - own_group * local_count
    own_parts = page_partials(
        keys_pool[:OWNED_SLOTS],
        values_pool[:OWNED_SLOTS],
        decay_pool[:OWNED_SLOTS],
        page_fill[:OWNED_SLOTS],
        by_request_rows[own_request],
        head_count,
    )
    hosted_request = page_request[OWNED_SLOTS:]
    hosted_owner = hosted_request // local_count
    hosted_local = hosted_request % local_count
    hosted_index = jnp.arange(hosted_request.shape[0])
    earlier = (hosted_owner[:, None] == hosted_owner[None, :]) & (
        hosted_index[None, :] < hosted_index[:, None]
    )
    hosted_rank = jnp.sum(earlier, axis=1)
    slot_match = (hosted_owner[None, None, :] == jnp.arange(groups)[:, None, None]) & (
        hosted_rank[None, None, :] == jnp.arange(capacity)[None, :, None]
    )
    slot_full = jnp.any(slot_match, axis=2)
    slot_source = jnp.sum(jnp.where(slot_match, hosted_index[None, None, :], 0), axis=2)
    slot_local = jnp.sum(jnp.where(slot_match, hosted_local[None, None, :], 0), axis=2)
    slot_count = groups * capacity
    base_rows = jnp.arange(row_count) // BEAMS * BEAMS
    hist_keys = jnp.zeros((0, row_count, inner_width), jnp.bfloat16)
    hist_values = jnp.zeros((0, row_count, inner_width), jnp.bfloat16)
    hist_totals = jnp.zeros((0, row_count, head_count), jnp.float32)
    running = jnp.zeros((row_count, head_count), jnp.float32)
    finished = []
    for step_index in range(step_count):
        query_block = by_row[:, step_index : step_index + 1]
        step_span = query_block.shape[1]
        gathered = lax.all_gather(query_block, "group", axis=0, tiled=True)
        asked_rows = gathered.reshape(groups * local_count, BEAMS, step_span, inner_width)[
            hosted_request
        ]
        page_top, page_total, numerator = page_partials(
            keys_pool[OWNED_SLOTS:],
            values_pool[OWNED_SLOTS:],
            decay_pool[OWNED_SLOTS:],
            page_fill[OWNED_SLOTS:],
            asked_rows,
            head_count,
        )
        full_slot = slot_full[:, :, None, None, None]
        own_now = tuple((member[:, :, step_index : step_index + 1] for member in own_parts))
        all_request = jnp.concatenate(
            [
                own_request,
                lax.all_to_all(
                    slot_local.astype(jnp.float32), "group", split_axis=0, concat_axis=0, tiled=True
                )
                .reshape(slot_count)
                .astype(jnp.int32),
            ],
            axis=0,
        )
        all_top = jnp.concatenate(
            [
                own_now[0],
                lax.all_to_all(
                    jnp.where(full_slot, page_top[slot_source], masked_score),
                    "group",
                    split_axis=0,
                    concat_axis=0,
                    tiled=True,
                ).reshape((slot_count,) + page_top.shape[1:]),
            ],
            axis=0,
        )
        all_total = jnp.concatenate(
            [
                own_now[1],
                lax.all_to_all(
                    jnp.where(full_slot, page_total[slot_source], 0.0),
                    "group",
                    split_axis=0,
                    concat_axis=0,
                    tiled=True,
                ).reshape((slot_count,) + page_total.shape[1:]),
            ],
            axis=0,
        )
        all_numer = jnp.concatenate(
            [
                own_now[2],
                lax.all_to_all(
                    jnp.where(full_slot, numerator[slot_source], 0.0),
                    "group",
                    split_axis=0,
                    concat_axis=0,
                    tiled=True,
                ).reshape((slot_count,) + numerator.shape[1:]),
            ],
            axis=0,
        )
        page_top, page_total, page_numer = by_request(
            all_request, all_top, all_total, all_numer, local_count, head_count
        )
        page_top = page_top.reshape(row_count, head_count)
        page_total = page_total.reshape(row_count, head_count)
        page_numer = page_numer.reshape(row_count, head_count, head_size)
        if step_index > 0:
            source = base_rows + parents[step_index - 1]
            hist_keys = hist_keys[:, source]
            hist_values = hist_values[:, source]
            hist_totals = hist_totals[:, source]
            running = running[source]
        running = running + forget[step_index]
        hist_keys = jnp.concatenate([hist_keys, key_new[step_index][None]], axis=0)
        hist_values = jnp.concatenate([hist_values, value_new[step_index][None]], axis=0)
        hist_totals = jnp.concatenate([hist_totals, running[None]], axis=0)
        asked_now = queries[step_index].reshape(row_count, head_count, head_size)
        keys_now = hist_keys.reshape(step_index + 1, row_count, head_count, head_size)
        values_now = hist_values.reshape(step_index + 1, row_count, head_count, head_size)
        scores = jnp.einsum(
            "rhd,urhd->rhu", asked_now, keys_now, preferred_element_type=jnp.float32
        ) * head_size ** (-0.5) - hist_totals.transpose(1, 2, 0)
        history_top = jnp.max(scores, axis=-1)
        weights = jnp.exp(scores - history_top[..., None])
        history_total = jnp.sum(weights, axis=-1)
        history_numer = jnp.einsum(
            "rhu,urhd->rhd",
            weights.astype(jnp.bfloat16),
            values_now,
            preferred_element_type=jnp.float32,
        )
        best_top = jnp.maximum(page_top, history_top)
        page_scale = jnp.exp(page_top - best_top)
        history_scale = jnp.exp(history_top - best_top)
        total_sum = page_total * page_scale + history_total * history_scale
        numer_sum = page_numer * page_scale[..., None] + history_numer * history_scale[..., None]
        attended = (
            (numer_sum / total_sum[..., None]).astype(jnp.bfloat16).reshape(row_count, inner_width)
        )
        mixed_sum = lax.psum(jnp.dot(attended, w_out, preferred_element_type=jnp.float32), "head")
        residual = tokens[step_index].astype(jnp.float32) + mixed_sum
        normed_ffn = rms_scale(residual, gain_ffn).astype(jnp.bfloat16)
        gate_proj = jnp.dot(normed_ffn, w_gate, preferred_element_type=jnp.float32)
        up_proj = jnp.dot(normed_ffn, w_up, preferred_element_type=jnp.float32)
        hidden = (jax.nn.silu(gate_proj) * up_proj).astype(jnp.bfloat16)
        down_sum = lax.psum(jnp.dot(hidden, w_down, preferred_element_type=jnp.float32), "head")
        finished.append((residual + down_sum).astype(jnp.bfloat16))
    result = jnp.stack(finished, axis=0)
    return result


def solution(mesh):
    return jax.shard_map(
        shards,
        mesh=mesh,
        in_specs=(
            P(None, "group", None),
            P(None, "group"),
            P("group"),
            P("group"),
            P("group", "head", None),
            P("group", "head", None),
            P("group", "head", None),
            P(),
            P("head", None),
            P("head", None),
            P("head", None),
            P(None, "head"),
            P("head"),
            P("head", None),
            P(),
            P(None, "head"),
            P(None, "head"),
            P("head", None),
        ),
        out_specs=P(None, "group", None),
        check_vma=False,
    )
```

profile of v0, /device:TPU:1, one launch (start us, length us, event | category | flops | bytes accessed | tf_op | source)
XLA Modules:
  0.0 839.9 jit_solution(794505036848824269)
XLA Ops:
  19.0 11.5 %all-to-all-start = ((f32[32,1,1]{2,1,0:T(1,128)}), f32[32,1,1]{2,1,0:T(1,128)}, u32[]{:S(2)}, u32[]{:S(2)}) async-start(f32[32,1,1]{2,1,0:T(1,128)} %copy.715), calls=%async_computation | async-start | bytes 32768 | tf_op jit(solution)/shard_map/all_to_all | solution.py:152
  56.5 4.7 copy.728
  61.2 4.6 reshape.1155
  179.1 67.7 %all-gather.11.cloned.1.call-done = bf16[4096,1,384]{2,0,1:T(8,128)(2,1)} async-done(((bf16[128,1,384]{2,0,1:T(8,128)(2,1)}), bf16[4096,1,384]{2,0,1:T(8,128)(2,1)}) %all-gather.11.cloned.1.call-update) | async-done | bytes 3145744 | tf_op jit(solution)/shard_map/all_gather | solution.py:135
  277.1 46.8 %all-gather.5.cloned.1.call-done = bf16[4096,1,384]{2,0,1:T(8,128)(2,1)} async-done(((bf16[128,1,384]{2,0,1:T(8,128)(2,1)}), bf16[4096,1,384]{2,0,1:T(8,128)(2,1)}) %all-gather.5.cloned.1.call-update) | async-done | bytes 3145744 | tf_op jit(solution)/shard_map/all_gather | solution.py:135
  372.1 5.6 all-to-all-start.1
  400.3 9.2 %all-to-all-start.4 = ((f32[32,1,8,1,6]{2,3,4,1,0:T(1,128)}), f32[32,1,8,1,6]{2,3,4,1,0:T(1,128)S(1)}, u32[]{:S(2)}, u32[]{:S(2)}) async-start(f32[32,1,8,1,6]{2,3,4,1,0:T(1,128)} %copy.745), calls=%async_computation.4 | async-start | bytes 196608 | tf_op jit(solution)/shard_map/all_to_all | solution.py:163
  418.4 8.4 all-to-all-start.7
  426.9 8.7 %all-to-all-done.7 = f32[32,1,8,1,6]{2,3,4,1,0:T(1,128)S(1)} async-done(((f32[32,1,8,1,6]{2,3,4,1,0:T(1,128)}), f32[32,1,8,1,6]{2,3,4,1,0:T(1,128)S(1)}, u32[]{:S(2)}, u32[]{:S(2)}) %all-to-all-start.7) | async-done | bytes 6176 | tf_op jit(solution)/shard_map/all_to_all | solution.py:163
  441.5 6.9 all-to-all-done.10
  453.8 7.3 all-to-all-done.3
  465.9 8.0 all-to-all-done.12
  481.4 5.9 all-to-all-done.6
  503.8 9.2 %all-to-all-start.2 = ((f32[32,1,8,1,384]{4,2,3,1,0:T(8,128)}), f32[32,1,8,1,384]{4,2,3,1,0:T(8,128)S(1)}, u32[]{:S(2)}, u32[]{:S(2)}) async-start(f32[32,1,8,1,384]{4,2,3,1,0:T(8,128)} %get-tuple-element.103), calls=%async_computation.2 | async-start | bytes 786432 | tf_op jit(solution)/shard_map/all_to_all | solution.py:189
  530.5 7.8 exponential_select_fusion.1
  539.5 9.3 %all-to-all-start.5 = ((f32[32,1,8,1,384]{4,2,3,1,0:T(8,128)}), f32[32,1,8,1,384]{4,2,3,1,0:T(8,128)}, u32[]{:S(2)}, u32[]{:S(2)}) async-start(f32[32,1,8,1,384]{4,2,3,1,0:T(8,128)} %get-tuple-element.101), calls=%async_computation.5 | async-start | bytes 786432 | tf_op jit(solution)/shard_map/all_to_all | solution.py:189
  552.9 7.7 multiply_reduce_fusion.3
  561.9 9.2 %all-to-all-start.11 = ((f32[32,1,8,1,384]{4,2,3,1,0:T(8,128)}), f32[32,1,8,1,384]{4,2,3,1,0:T(8,128)S(1)}, u32[]{:S(2)}, u32[]{:S(2)}) async-start(f32[32,1,8,1,384]{4,2,3,1,0:T(8,128)} %get-tuple-element.102), calls=%async_computation.11 | async-start | bytes 786432 | tf_op jit(solution)/shard_map/all_to_all | solution.py:189
  577.7 7.7 multiply_reduce_fusion.2
  590.9 9.3 %all-to-all-start.8 = ((f32[32,1,8,1,384]{4,2,3,1,0:T(8,128)}), f32[32,1,8,1,384]{4,2,3,1,0:T(8,128)}, u32[]{:S(2)}, u32[]{:S(2)}) async-start(f32[32,1,8,1,384]{4,2,3,1,0:T(8,128)} %get-tuple-element.100), calls=%async_computation.8 | async-start | bytes 786432 | tf_op jit(solution)/shard_map/all_to_all | solution.py:189
  604.5 7.7 multiply_reduce_fusion
  620.3 7.7 multiply_reduce_fusion.1
  631.2 88.7 %all-reduce.7.cloned.1.call-done = (f32[128,1536]{1,0:T(8,128)}, f32[128,1536]{1,0:T(8,128)}, f32[128,1536]{1,0:T(8,128)}, f32[128,1536]{1,0:T(8,128)}) async-done(((f32[128,1536]{1,0:T(8,128)}, f32[128,1536]{1,0:T(8,128)}, f32[128,1536]{1,0:T(8,128)}, f32[128,1536]{1,0:T(8,128)}), (f32[128,1536]{1,0:T(8,128)}, f32[128,1536]{1,0:T(8,128)}, f32[128,1536]{1,0:T(8,128)}, ...) | async-done | bytes 3145744 | tf_op jit(solution)/shard_map/psum | solution.py:238
  751.3 76.1 %all-reduce.5.cloned.1.call-done = (f32[128,1536]{1,0:T(8,128)}, f32[128,1536]{1,0:T(8,128)}, f32[128,1536]{1,0:T(8,128)}, f32[128,1536]{1,0:T(8,128)}) async-done(((f32[128,1536]{1,0:T(8,128)}, f32[128,1536]{1,0:T(8,128)}, f32[128,1536]{1,0:T(8,128)}, f32[128,1536]{1,0:T(8,128)}), (f32[128,1536]{1,0:T(8,128)}, f32[128,1536]{1,0:T(8,128)}, f32[128,1536]{1,0:T(8,128)}, ...) | async-done | bytes 3145744 | tf_op jit(solution)/shard_map/psum | solution.py:244
  (487 shorter events, 389.3 us)
Async XLA Ops:
  6.5 721.9 %copy-start = (bf16[1024,1536]{1,0:T(8,128)(2,1)S(1)}, bf16[1024,1536]{1,0:T(8,128)(2,1)}, u32[]{:S(2)}) copy-start(bf16[1024,1536]{1,0:T(8,128)(2,1)} %param.35) | copy-start | bytes 9437188
  6.5 165.9 %all-gather.9.cloned.1.call-start = ((), (), s32[]{:S(2)}) async-start(), calls=%async_computation.15 | async-start | bytes 3244032 | tf_op jit(solution)/shard_map/all_gather | solution.py:135
  15.1 160.7 %all-gather.7.cloned.1.call-start = ((), (), s32[]{:S(2)}) async-start(), calls=%async_computation.14 | async-start | bytes 3244032 | tf_op jit(solution)/shard_map/all_gather | solution.py:135
  15.8 231.1 %all-gather.11.cloned.1.call-start = ((), (), s32[]{:S(2)}) async-start(), calls=%async_computation.16 | async-start | bytes 3244032 | tf_op jit(solution)/shard_map/all_gather | solution.py:135
  19.0 150.7 %all-to-all-start = ((f32[32,1,1]{2,1,0:T(1,128)}), f32[32,1,1]{2,1,0:T(1,128)}, u32[]{:S(2)}, u32[]{:S(2)}) async-start(f32[32,1,1]{2,1,0:T(1,128)} %copy.715), calls=%async_computation | async-start | bytes 32768 | tf_op jit(solution)/shard_map/all_to_all | solution.py:152
  30.4 293.4 %all-gather.5.cloned.1.call-start = ((), (), s32[]{:S(2)}) async-start(), calls=%async_computation.13 | async-start | bytes 3244032 | tf_op jit(solution)/shard_map/all_gather | solution.py:135
  166.1 226.7 %copy-start.56 = (s32[1024]{0:T(1024)}, s32[1024]{0:T(1024)S(1)}, u32[]{:S(2)}) copy-start(s32[1024]{0:T(1024)S(1)} %pad_clamp_fusion.3) | copy-start | bytes 12292
  372.1 28.2 %all-to-all-start.1 = ((f32[32,1,8,1,6]{2,3,4,1,0:T(1,128)}), f32[32,1,8,1,6]{2,3,4,1,0:T(1,128)}, u32[]{:S(2)}, u32[]{:S(2)}) async-start(f32[32,1,8,1,6]{2,3,4,1,0:T(1,128)} %copy.724), calls=%async_computation.1 | async-start | bytes 196608 | tf_op jit(solution)/shard_map/all_to_all | solution.py:163
  400.3 18.1 %all-to-all-start.4 = ((f32[32,1,8,1,6]{2,3,4,1,0:T(1,128)}), f32[32,1,8,1,6]{2,3,4,1,0:T(1,128)S(1)}, u32[]{:S(2)}, u32[]{:S(2)}) async-start(f32[32,1,8,1,6]{2,3,4,1,0:T(1,128)} %copy.745), calls=%async_computation.4 | async-start | bytes 196608 | tf_op jit(solution)/shard_map/all_to_all | solution.py:163
  418.4 17.3 %all-to-all-start.7 = ((f32[32,1,8,1,6]{2,3,4,1,0:T(1,128)}), f32[32,1,8,1,6]{2,3,4,1,0:T(1,128)S(1)}, u32[]{:S(2)}, u32[]{:S(2)}) async-start(f32[32,1,8,1,6]{2,3,4,1,0:T(1,128)} %copy.771), calls=%async_computation.7 | async-start | bytes 196608 | tf_op jit(solution)/shard_map/all_to_all | solution.py:163
  426.9 76.8 %copy-start.34 = (f32[64,8,6]{0,1,2:T(8,128)}, f32[64,8,6]{0,1,2:T(8,128)S(1)}, u32[]{:S(2)}) copy-start(f32[64,8,6]{0,1,2:T(8,128)S(1)} %get-tuple-element.124) | copy-start | bytes 36868
  435.6 12.7 %all-to-all-start.10 = ((f32[32,1,8,1,6]{2,3,4,1,0:T(1,128)}), f32[32,1,8,1,6]{2,3,4,1,0:T(1,128)S(1)}, u32[]{:S(2)}, u32[]{:S(2)}) async-start(f32[32,1,8,1,6]{2,3,4,1,0:T(1,128)} %copy.803), calls=%async_computation.10 | async-start | bytes 196608 | tf_op jit(solution)/shard_map/all_to_all | solution.py:163
  440.8 62.9 %copy-start.27 = (f32[16,8,6]{1,2,0:T(8,128)}, f32[16,8,6]{1,2,0:T(8,128)S(1)}, u32[]{:S(2)}) copy-start(f32[16,8,6]{1,2,0:T(8,128)S(1)} %select_reduce_fusion.3) | copy-start | bytes 9220
  448.4 12.7 %all-to-all-start.3 = ((f32[32,1,8,1,6]{2,3,4,1,0:T(1,128)}), f32[32,1,8,1,6]{2,3,4,1,0:T(1,128)S(1)}, u32[]{:S(2)}, u32[]{:S(2)}) async-start(f32[32,1,8,1,6]{2,3,4,1,0:T(1,128)} %copy.737), calls=%async_computation.3 | async-start | bytes 196608 | tf_op jit(solution)/shard_map/all_to_all | solution.py:176
  461.1 12.8 %all-to-all-start.12 = ((f32[32,1,8,1,6]{2,3,4,1,0:T(1,128)}), f32[32,1,8,1,6]{2,3,4,1,0:T(1,128)S(1)}, u32[]{:S(2)}, u32[]{:S(2)}) async-start(f32[32,1,8,1,6]{2,3,4,1,0:T(1,128)} %copy.826), calls=%async_computation.12 | async-start | bytes 196608 | tf_op jit(solution)/shard_map/all_to_all | solution.py:176
  473.9 13.4 %all-to-all-start.6 = ((f32[32,1,8,1,6]{2,3,4,1,0:T(1,128)}), f32[32,1,8,1,6]{2,3,4,1,0:T(1,128)}, u32[]{:S(2)}, u32[]{:S(2)}) async-start(f32[32,1,8,1,6]{2,3,4,1,0:T(1,128)} %copy.763), calls=%async_computation.6 | async-start | bytes 196608 | tf_op jit(solution)/shard_map/all_to_all | solution.py:176
  487.3 16.4 %all-to-all-start.9 = ((f32[32,1,8,1,6]{2,3,4,1,0:T(1,128)}), f32[32,1,8,1,6]{2,3,4,1,0:T(1,128)}, u32[]{:S(2)}, u32[]{:S(2)}) async-start(f32[32,1,8,1,6]{2,3,4,1,0:T(1,128)} %copy.794), calls=%async_computation.9 | async-start | bytes 196608 | tf_op jit(solution)/shard_map/all_to_all | solution.py:176
  503.8 35.7 %all-to-all-start.2 = ((f32[32,1,8,1,384]{4,2,3,1,0:T(8,128)}), f32[32,1,8,1,384]{4,2,3,1,0:T(8,128)S(1)}, u32[]{:S(2)}, u32[]{:S(2)}) async-start(f32[32,1,8,1,384]{4,2,3,1,0:T(8,128)} %get-tuple-element.103), calls=%async_computation.2 | async-start | bytes 786432 | tf_op jit(solution)/shard_map/all_to_all | solution.py:189
  539.5 22.4 %all-to-all-start.5 = ((f32[32,1,8,1,384]{4,2,3,1,0:T(8,128)}), f32[32,1,8,1,384]{4,2,3,1,0:T(8,128)}, u32[]{:S(2)}, u32[]{:S(2)}) async-start(f32[32,1,8,1,384]{4,2,3,1,0:T(8,128)} %get-tuple-element.101), calls=%async_computation.5 | async-start | bytes 786432 | tf_op jit(solution)/shard_map/all_to_all | solution.py:189
  561.9 28.9 %all-to-all-start.11 = ((f32[32,1,8,1,384]{4,2,3,1,0:T(8,128)}), f32[32,1,8,1,384]{4,2,3,1,0:T(8,128)S(1)}, u32[]{:S(2)}, u32[]{:S(2)}) async-start(f32[32,1,8,1,384]{4,2,3,1,0:T(8,128)} %get-tuple-element.102), calls=%async_computation.11 | async-start | bytes 786432 | tf_op jit(solution)/shard_map/all_to_all | solution.py:189
  590.9 24.4 %all-to-all-start.8 = ((f32[32,1,8,1,384]{4,2,3,1,0:T(8,128)}), f32[32,1,8,1,384]{4,2,3,1,0:T(8,128)}, u32[]{:S(2)}, u32[]{:S(2)}) async-start(f32[32,1,8,1,384]{4,2,3,1,0:T(8,128)} %get-tuple-element.100), calls=%async_computation.8 | async-start | bytes 786432 | tf_op jit(solution)/shard_map/all_to_all | solution.py:189
  600.2 119.6 %all-reduce.7.cloned.1.call-start = ((), (), s32[]{:S(2)}) async-start(), calls=%async_computation.18 | async-start | bytes 6291456 | tf_op jit(solution)/shard_map/psum | solution.py:238
  631.1 91.7 %copy-start.76 = (f32[1536]{0:T(1024)S(1)}, f32[1536]{0:T(1024)}, u32[]{:S(2)}) copy-start(f32[1536]{0:T(1024)} %param.32) | copy-start | bytes 18436
  631.1 196.3 %all-reduce.5.cloned.1.call-start = ((), (), s32[]{:S(2)}) async-start(), calls=%async_computation.17 | async-start | bytes 6291456 | tf_op jit(solution)/shard_map/psum | solution.py:244
  (87 other events, 964.8 us)
Sparse Core Ops, SparseCore 0:
  15.2 77.4 all-gather.8
  95.7 74.0 all-gather.6
  172.8 74.0 all-gather.10
  249.7 74.0 all-gather.4
  631.3 88.5 all-reduce.6
  751.5 75.9 all-reduce.4
where the time goes:
time: 854 us; the launch traced here: 840 us
  waiting for transfers between devices  319 us (37%)
  local copies, waits for them, and re-layouts  223 us (26%)
  other arithmetic  123 us (14%)
  starting transfers between devices  93.1 us (11%)
  matrix products  66.5 us (8%)
  between operations  14.9 us (2%)
    all_gather x4, waiting for transfers between devices, shards(): gathered = lax.all_gather(query_block, 'group', axis=0, tiled=True)  115 us
    psum x1, waiting for transfers between devices, shards(): lax.psum(jnp.dot(attended, w_out, preferred_element_type=jnp.float32), 'h...  88.7 us
    psum x1, waiting for transfers between devices, shards(): lax.psum(jnp.dot(hidden, w_down, preferred_element_type=jnp.float32), 'he...  76.1 us
    all_to_all x4, starting transfers between devices, shards(): lax.all_to_all(jnp.where(full_slot, numerator[slot_source], 0.0), 'group'...  37 us
    reduce_sum x4, other arithmetic, by_request(): combined = jnp.sum(factor[..., None] * numer_split[None], axis=1)  30.9 us
    all_to_all x4, starting transfers between devices, shards(): lax.all_to_all(jnp.where(full_slot, page_top[slot_source], masked_score),...  27.4 us
    all_to_all x4, waiting for transfers between devices, shards(): lax.all_to_all(jnp.where(full_slot, page_total[slot_source], 0.0), 'group...  21.2 us
  transfers between devices with their start and end apart: 19, of which 11 were waited for; matrix products, arithmetic and copies ran while one was open for 36% of the time, Pallas kernels for 0%

commit v1 on v0

--- a/solution.py
+++ b/solution.py
@@ -241,7 +241,10 @@
         gate_proj = jnp.dot(normed_ffn, w_gate, preferred_element_type=jnp.float32)
         up_proj = jnp.dot(normed_ffn, w_up, preferred_element_type=jnp.float32)
         hidden = (jax.nn.silu(gate_proj) * up_proj).astype(jnp.bfloat16)
-        down_sum = lax.psum(jnp.dot(hidden, w_down, preferred_element_type=jnp.float32), "head")
+        down_sum = jnp.sum(
+            lax.all_gather(jnp.dot(hidden, w_down, preferred_element_type=jnp.float32), "head"),
+            axis=0,
+        )
         finished.append((residual + down_sum).astype(jnp.bfloat16))
     result = jnp.stack(finished, axis=0)
     return result

time: 854 us -> 921 us (1.078)
  waiting for transfers between devices: 319 us -> 371 us
  other arithmetic: 123 us -> 136 us
    all_gather x0 -> x4, waiting for transfers between devices: none -> 128 us  [shards(): lax.all_gather(jnp.dot(hidden, w_down, preferred_element_type=jnp.float32...]
    psum x1 -> x0, waiting for transfers between devices: 76.1 us -> none  [shards(): lax.psum(jnp.dot(hidden, w_down, preferred_element_type=jnp.float32), 'he...]
    reduce_sum x0 -> x4, other arithmetic: none -> 12.4 us  [shards(): jnp.sum(lax.all_gather(jnp.dot(hidden, w_down, preferred_element_type=jnp...]
  transfers between devices with their start and end apart: 19 -> 22, of which waited for: 11 -> 14; matrix products, arithmetic and copies ran while one was open for 36% -> 37% of each run, Pallas kernels for 0% -> 0%
where the time goes in v1:
time: 921 us; the launch traced here: 907 us
  waiting for transfers between devices  371 us (40%)
  local copies, waits for them, and re-layouts  224 us (24%)
  other arithmetic  136 us (15%)
  starting transfers between devices  93.3 us (10%)
  matrix products  68.9 us (7%)
  between operations  14.9 us (2%)
    all_gather x4, waiting for transfers between devices, shards(): lax.all_gather(jnp.dot(hidden, w_down, preferred_element_type=jnp.float32...  128 us
    all_gather x4, waiting for transfers between devices, shards(): gathered = lax.all_gather(query_block, 'group', axis=0, tiled=True)  114 us
    psum x1, waiting for transfers between devices, shards(): lax.psum(jnp.dot(attended, w_out, preferred_element_type=jnp.float32), 'h...  88.7 us
    all_to_all x4, starting transfers between devices, shards(): lax.all_to_all(jnp.where(full_slot, numerator[slot_source], 0.0), 'group'...  37 us
    reduce_sum x4, other arithmetic, by_request(): combined = jnp.sum(factor[..., None] * numer_split[None], axis=1)  30.9 us
    all_to_all x4, starting transfers between devices, shards(): lax.all_to_all(jnp.where(full_slot, page_top[slot_source], masked_score),...  27.1 us
    all_to_all x4, waiting for transfers between devices, shards(): lax.all_to_all(jnp.where(full_slot, page_total[slot_source], 0.0), 'group...  21.2 us
  transfers between devices with their start and end apart: 22, of which 14 were waited for; matrix products, arithmetic and copies ran while one was open for 37% of the time, Pallas kernels for 0%

profile of v1, /device:TPU:1, one launch (start us, length us, event | category | flops | bytes accessed | tf_op | source)
XLA Modules:
  0.0 907.2 jit_solution(17637661946772282779)
XLA Ops:
  19.1 11.5 %all-to-all-start = ((f32[32,1,1]{2,1,0:T(1,128)}), f32[32,1,1]{2,1,0:T(1,128)}, u32[]{:S(2)}, u32[]{:S(2)}) async-start(f32[32,1,1]{2,1,0:T(1,128)} %copy.715), calls=%async_computation | async-start | bytes 32768 | tf_op jit(solution)/shard_map/all_to_all | solution.py:152
  179.7 67.2 %all-gather.19.cloned.1.call-done = bf16[4096,1,384]{2,0,1:T(8,128)(2,1)} async-done(((bf16[128,1,384]{2,0,1:T(8,128)(2,1)}), bf16[4096,1,384]{2,0,1:T(8,128)(2,1)}) %all-gather.19.cloned.1.call-update) | async-done | bytes 3145744 | tf_op jit(solution)/shard_map/all_gather | solution.py:135
  277.1 46.7 %all-gather.13.cloned.1.call-done = bf16[4096,1,384]{2,0,1:T(8,128)(2,1)} async-done(((bf16[128,1,384]{2,0,1:T(8,128)(2,1)}), bf16[4096,1,384]{2,0,1:T(8,128)(2,1)}) %all-gather.13.cloned.1.call-update) | async-done | bytes 3145744 | tf_op jit(solution)/shard_map/all_gather | solution.py:135
  400.4 9.2 %all-to-all-start.4 = ((f32[32,1,8,1,6]{2,3,4,1,0:T(1,128)}), f32[32,1,8,1,6]{2,3,4,1,0:T(1,128)S(1)}, u32[]{:S(2)}, u32[]{:S(2)}) async-start(f32[32,1,8,1,6]{2,3,4,1,0:T(1,128)} %copy.745), calls=%async_computation.4 | async-start | bytes 196608 | tf_op jit(solution)/shard_map/all_to_all | solution.py:163
  418.5 8.4 all-to-all-start.7
  427.1 8.7 all-to-all-done.7
  441.3 7.2 all-to-all-done.10
  454.0 7.3 all-to-all-done.3
  466.1 8.0 all-to-all-done.12
  481.6 5.9 all-to-all-done.6
  504.0 9.2 %all-to-all-start.2 = ((f32[32,1,8,1,384]{4,2,3,1,0:T(8,128)}), f32[32,1,8,1,384]{4,2,3,1,0:T(8,128)S(1)}, u32[]{:S(2)}, u32[]{:S(2)}) async-start(f32[32,1,8,1,384]{4,2,3,1,0:T(8,128)} %get-tuple-element.99), calls=%async_computation.2 | async-start | bytes 786432 | tf_op jit(solution)/shard_map/all_to_all | solution.py:189
  530.7 7.8 exponential_select_fusion.1
  539.8 9.3 %all-to-all-start.5 = ((f32[32,1,8,1,384]{4,2,3,1,0:T(8,128)}), f32[32,1,8,1,384]{4,2,3,1,0:T(8,128)}, u32[]{:S(2)}, u32[]{:S(2)}) async-start(f32[32,1,8,1,384]{4,2,3,1,0:T(8,128)} %get-tuple-element.97), calls=%async_computation.5 | async-start | bytes 786432 | tf_op jit(solution)/shard_map/all_to_all | solution.py:189
  553.2 7.7 multiply_reduce_fusion.3
  562.2 9.2 %all-to-all-start.11 = ((f32[32,1,8,1,384]{4,2,3,1,0:T(8,128)}), f32[32,1,8,1,384]{4,2,3,1,0:T(8,128)S(1)}, u32[]{:S(2)}, u32[]{:S(2)}) async-start(f32[32,1,8,1,384]{4,2,3,1,0:T(8,128)} %get-tuple-element.98), calls=%async_computation.11 | async-start | bytes 786432 | tf_op jit(solution)/shard_map/all_to_all | solution.py:189
  578.0 7.7 multiply_reduce_fusion.2
  591.1 9.3 %all-to-all-start.8 = ((f32[32,1,8,1,384]{4,2,3,1,0:T(8,128)}), f32[32,1,8,1,384]{4,2,3,1,0:T(8,128)}, u32[]{:S(2)}, u32[]{:S(2)}) async-start(f32[32,1,8,1,384]{4,2,3,1,0:T(8,128)} %get-tuple-element.96), calls=%async_computation.8 | async-start | bytes 786432 | tf_op jit(solution)/shard_map/all_to_all | solution.py:189
  604.7 7.7 multiply_reduce_fusion
  620.6 7.7 multiply_reduce_fusion.1
  631.5 88.7 %all-reduce.3.cloned.1.call-done = (f32[128,1536]{1,0:T(8,128)}, f32[128,1536]{1,0:T(8,128)}, f32[128,1536]{1,0:T(8,128)}, f32[128,1536]{1,0:T(8,128)}) async-done(((f32[128,1536]{1,0:T(8,128)}, f32[128,1536]{1,0:T(8,128)}, f32[128,1536]{1,0:T(8,128)}, f32[128,1536]{1,0:T(8,128)}), (f32[128,1536]{1,0:T(8,128)}, f32[128,1536]{1,0:T(8,128)}, f32[128,1536]{1,0:T(8,128)}, ...) | async-done | bytes 3145744 | tf_op jit(solution)/shard_map/psum | solution.py:238
  754.6 16.0 %all-gather.21.cloned.1.call-done = f32[512,1536]{1,0:T(8,128)} async-done(((f32[128,1536]{1,0:T(8,128)}), f32[512,1536]{1,0:T(8,128)}) %all-gather.21.cloned.1.call-update) | async-done | bytes 3145744 | tf_op jit(solution)/shard_map/all_gather | solution.py:245
  773.6 37.3 %all-gather.25.cloned.1.call-done = f32[512,1536]{1,0:T(8,128)} async-done(((f32[128,1536]{1,0:T(8,128)}), f32[512,1536]{1,0:T(8,128)}) %all-gather.25.cloned.1.call-update) | async-done | bytes 3145744 | tf_op jit(solution)/shard_map/all_gather | solution.py:245
  814.0 37.3 %all-gather.23.cloned.1.call-done = f32[512,1536]{1,0:T(8,128)} async-done(((f32[128,1536]{1,0:T(8,128)}), f32[512,1536]{1,0:T(8,128)}) %all-gather.23.cloned.1.call-update) | async-done | bytes 3145744 | tf_op jit(solution)/shard_map/all_gather | solution.py:245
  854.4 37.3 %all-gather.27.cloned.1.call-done = f32[512,1536]{1,0:T(8,128)} async-done(((f32[128,1536]{1,0:T(8,128)}), f32[512,1536]{1,0:T(8,128)}) %all-gather.27.cloned.1.call-update) | async-done | bytes 3145744 | tf_op jit(solution)/shard_map/all_gather | solution.py:245
  (498 shorter events, 420.0 us)
Async XLA Ops:
  6.5 720.9 %copy-start = (bf16[1024,1536]{1,0:T(8,128)(2,1)S(1)}, bf16[1024,1536]{1,0:T(8,128)(2,1)}, u32[]{:S(2)}) copy-start(bf16[1024,1536]{1,0:T(8,128)(2,1)} %param.35) | copy-start | bytes 9437188
  6.5 166.4 %all-gather.17.cloned.1.call-start = ((), (), s32[]{:S(2)}) async-start(), calls=%async_computation.15 | async-start | bytes 3244032 | tf_op jit(solution)/shard_map/all_gather | solution.py:135
  15.1 161.3 %all-gather.15.cloned.1.call-start = ((), (), s32[]{:S(2)}) async-start(), calls=%async_computation.14 | async-start | bytes 3244032 | tf_op jit(solution)/shard_map/all_gather | solution.py:135
  15.8 231.1 %all-gather.19.cloned.1.call-start = ((), (), s32[]{:S(2)}) async-start(), calls=%async_computation.16 | async-start | bytes 3244032 | tf_op jit(solution)/shard_map/all_gather | solution.py:135
  19.1 151.2 %all-to-all-start = ((f32[32,1,1]{2,1,0:T(1,128)}), f32[32,1,1]{2,1,0:T(1,128)}, u32[]{:S(2)}, u32[]{:S(2)}) async-start(f32[32,1,1]{2,1,0:T(1,128)} %copy.715), calls=%async_computation | async-start | bytes 32768 | tf_op jit(solution)/shard_map/all_to_all | solution.py:152
  30.6 293.3 %all-gather.13.cloned.1.call-start = ((), (), s32[]{:S(2)}) async-start(), calls=%async_computation.13 | async-start | bytes 3244032 | tf_op jit(solution)/shard_map/all_gather | solution.py:135
  166.5 226.3 %copy-start.55 = (s32[1024]{0:T(1024)}, s32[1024]{0:T(1024)S(1)}, u32[]{:S(2)}) copy-start(s32[1024]{0:T(1024)S(1)} %pad_clamp_fusion.3) | copy-start | bytes 12292
  372.2 28.2 %all-to-all-start.1 = ((f32[32,1,8,1,6]{2,3,4,1,0:T(1,128)}), f32[32,1,8,1,6]{2,3,4,1,0:T(1,128)}, u32[]{:S(2)}, u32[]{:S(2)}) async-start(f32[32,1,8,1,6]{2,3,4,1,0:T(1,128)} %copy.724), calls=%async_computation.1 | async-start | bytes 196608 | tf_op jit(solution)/shard_map/all_to_all | solution.py:163
  400.4 18.1 %all-to-all-start.4 = ((f32[32,1,8,1,6]{2,3,4,1,0:T(1,128)}), f32[32,1,8,1,6]{2,3,4,1,0:T(1,128)S(1)}, u32[]{:S(2)}, u32[]{:S(2)}) async-start(f32[32,1,8,1,6]{2,3,4,1,0:T(1,128)} %copy.745), calls=%async_computation.4 | async-start | bytes 196608 | tf_op jit(solution)/shard_map/all_to_all | solution.py:163
  418.5 17.3 %all-to-all-start.7 = ((f32[32,1,8,1,6]{2,3,4,1,0:T(1,128)}), f32[32,1,8,1,6]{2,3,4,1,0:T(1,128)S(1)}, u32[]{:S(2)}, u32[]{:S(2)}) async-start(f32[32,1,8,1,6]{2,3,4,1,0:T(1,128)} %copy.771), calls=%async_computation.7 | async-start | bytes 196608 | tf_op jit(solution)/shard_map/all_to_all | solution.py:163
  435.8 12.7 %all-to-all-start.10 = ((f32[32,1,8,1,6]{2,3,4,1,0:T(1,128)}), f32[32,1,8,1,6]{2,3,4,1,0:T(1,128)S(1)}, u32[]{:S(2)}, u32[]{:S(2)}) async-start(f32[32,1,8,1,6]{2,3,4,1,0:T(1,128)} %copy.803), calls=%async_computation.10 | async-start | bytes 196608 | tf_op jit(solution)/shard_map/all_to_all | solution.py:163
  448.5 12.8 %all-to-all-start.3 = ((f32[32,1,8,1,6]{2,3,4,1,0:T(1,128)}), f32[32,1,8,1,6]{2,3,4,1,0:T(1,128)S(1)}, u32[]{:S(2)}, u32[]{:S(2)}) async-start(f32[32,1,8,1,6]{2,3,4,1,0:T(1,128)} %copy.737), calls=%async_computation.3 | async-start | bytes 196608 | tf_op jit(solution)/shard_map/all_to_all | solution.py:176
  461.3 12.8 %all-to-all-start.12 = ((f32[32,1,8,1,6]{2,3,4,1,0:T(1,128)}), f32[32,1,8,1,6]{2,3,4,1,0:T(1,128)S(1)}, u32[]{:S(2)}, u32[]{:S(2)}) async-start(f32[32,1,8,1,6]{2,3,4,1,0:T(1,128)} %copy.826), calls=%async_computation.12 | async-start | bytes 196608 | tf_op jit(solution)/shard_map/all_to_all | solution.py:176
  474.0 13.5 %all-to-all-start.6 = ((f32[32,1,8,1,6]{2,3,4,1,0:T(1,128)}), f32[32,1,8,1,6]{2,3,4,1,0:T(1,128)}, u32[]{:S(2)}, u32[]{:S(2)}) async-start(f32[32,1,8,1,6]{2,3,4,1,0:T(1,128)} %copy.763), calls=%async_computation.6 | async-start | bytes 196608 | tf_op jit(solution)/shard_map/all_to_all | solution.py:176
  487.5 16.5 %all-to-all-start.9 = ((f32[32,1,8,1,6]{2,3,4,1,0:T(1,128)}), f32[32,1,8,1,6]{2,3,4,1,0:T(1,128)}, u32[]{:S(2)}, u32[]{:S(2)}) async-start(f32[32,1,8,1,6]{2,3,4,1,0:T(1,128)} %copy.794), calls=%async_computation.9 | async-start | bytes 196608 | tf_op jit(solution)/shard_map/all_to_all | solution.py:176
  504.0 35.8 %all-to-all-start.2 = ((f32[32,1,8,1,384]{4,2,3,1,0:T(8,128)}), f32[32,1,8,1,384]{4,2,3,1,0:T(8,128)S(1)}, u32[]{:S(2)}, u32[]{:S(2)}) async-start(f32[32,1,8,1,384]{4,2,3,1,0:T(8,128)} %get-tuple-element.99), calls=%async_computation.2 | async-start | bytes 786432 | tf_op jit(solution)/shard_map/all_to_all | solution.py:189
  539.8 22.4 %all-to-all-start.5 = ((f32[32,1,8,1,384]{4,2,3,1,0:T(8,128)}), f32[32,1,8,1,384]{4,2,3,1,0:T(8,128)}, u32[]{:S(2)}, u32[]{:S(2)}) async-start(f32[32,1,8,1,384]{4,2,3,1,0:T(8,128)} %get-tuple-element.97), calls=%async_computation.5 | async-start | bytes 786432 | tf_op jit(solution)/shard_map/all_to_all | solution.py:189
  562.2 28.9 %all-to-all-start.11 = ((f32[32,1,8,1,384]{4,2,3,1,0:T(8,128)}), f32[32,1,8,1,384]{4,2,3,1,0:T(8,128)S(1)}, u32[]{:S(2)}, u32[]{:S(2)}) async-start(f32[32,1,8,1,384]{4,2,3,1,0:T(8,128)} %get-tuple-element.98), calls=%async_computation.11 | async-start | bytes 786432 | tf_op jit(solution)/shard_map/all_to_all | solution.py:189
  591.1 24.5 %all-to-all-start.8 = ((f32[32,1,8,1,384]{4,2,3,1,0:T(8,128)}), f32[32,1,8,1,384]{4,2,3,1,0:T(8,128)}, u32[]{:S(2)}, u32[]{:S(2)}) async-start(f32[32,1,8,1,384]{4,2,3,1,0:T(8,128)} %get-tuple-element.96), calls=%async_computation.8 | async-start | bytes 786432 | tf_op jit(solution)/shard_map/all_to_all | solution.py:189
  600.5 119.7 %all-reduce.3.cloned.1.call-start = ((), (), s32[]{:S(2)}) async-start(), calls=%async_computation.21 | async-start | bytes 6291456 | tf_op jit(solution)/shard_map/psum | solution.py:238
  631.5 139.1 %all-gather.21.cloned.1.call-start = ((), (), s32[]{:S(2)}) async-start(), calls=%async_computation.17 | async-start | bytes 3932160 | tf_op jit(solution)/shard_map/all_gather | solution.py:245
  731.6 79.4 %all-gather.25.cloned.1.call-start = ((), (), s32[]{:S(2)}) async-start(), calls=%async_computation.19 | async-start | bytes 3932160 | tf_op jit(solution)/shard_map/all_gather | solution.py:245
  739.1 112.2 %all-gather.23.cloned.1.call-start = ((), (), s32[]{:S(2)}) async-start(), calls=%async_computation.18 | async-start | bytes 3932160 | tf_op jit(solution)/shard_map/all_gather | solution.py:245
  747.0 144.7 %all-gather.27.cloned.1.call-start = ((), (), s32[]{:S(2)}) async-start(), calls=%async_computation.20 | async-start | bytes 3932160 | tf_op jit(solution)/shard_map/all_gather | solution.py:245
  (89 other events, 1196.2 us)
Sparse Core Ops, SparseCore 0:
  15.2 77.4 all-gather.16
  95.7 74.0 all-gather.14
  172.8 74.0 all-gather.18
  249.7 74.0 all-gather.12
  631.6 88.5 all-reduce.2
  731.7 38.8 all-gather.20
  772.2 38.6 all-gather.24
  812.6 38.6 all-gather.22
  853.0 38.6 all-gather.26
